TPU v7x, 256 devices: a whole 4x4x8 slice. The times are simulated.
256 devices in a mesh: tm: 32 (over y, z_hi, core), fiber: 8 (over x, z_lo).
Axes of the slice: x: 4, y: 4, z: 8 (z_hi: 4, z_lo: 2; z = z_hi * 2 + z_lo), core: 2. Of those that a mesh axis runs over, the one named last changes fastest.
Arguments:
- waveform: bfloat16 [4096, 65536], P('fiber', 'tm'), may hold values from -6 to 6
- filters: bfloat16 [512, 256], replicated, may hold values from -0.25 to 0.25
- channel_section: int32 [4096], replicated, may hold values from 0 to 127, never falling along the last dimension, each value on 1 to 64 neighbouring positions
- section_bank: int32 [128, 8], replicated, may hold values from 0 to 1
- conv_bank: bfloat16 [2, 8, 3, 3, 32, 32], P(None, 'fiber'), may hold values from -0.375 to 0.375
Outputs:
- events: bfloat16 [4096, 256, 512], P('tm', 'fiber')
Inputs may be any that keep to these rules, and one draw needn't show every extreme that they name: `channel_section`: never falls along the channels; every section has 1 to 64 channels.
All inputs are finite; a program needn't handle non-finite values.
Results may differ from a plain program's by a relative error of at most 0.005.
Values may be sent and summed in bfloat16 or wider, within the bound.
No kernel may reach another device: no remote copies, remote signals or barrier semaphores. Data moves between devices by JAX's collectives and lax.ppermute only.
A program may use at most 128 MiB of HBM per device.

v0:
```python
import math

import jax
import jax.numpy as jnp
from jax import lax
from jax.sharding import PartitionSpec as P

HOP = 128
GW = 32


def from_behind(block, axis, distance):
    devices = range(lax.axis_size(axis))
    route = [(i - distance, i) for i in devices if i - distance in devices]
    return lax.ppermute(block, axis, route)


def extended_2(x, sides, width):
    for axis, dim in sides:
        size, length = (lax.axis_size(axis), x.shape[dim])
        up = [(i, (i + 1) % size) for i in range(size - 1)]
        down = [(j, i) for i, j in up]
        last = lax.slice_in_dim(x, length - width, length, axis=dim)
        first = lax.slice_in_dim(x, 0, width, axis=dim)
        before = lax.ppermute(last, axis, up)
        after = lax.ppermute(first, axis, down)
        x = jnp.concatenate([before, x, after], axis=dim)
    return x


def shards(waveform, filters, channel_section, section_bank, conv_bank):
    ch_dev, samp_dev = waveform.shape
    taps, nfilt = filters.shape
    frames_dev = samp_dev // HOP
    groups = nfilt // GW
    rim = from_behind(waveform[:, : taps - HOP], "tm", -1)
    extended = jnp.concatenate([waveform, rim], axis=1)
    blocks = extended.reshape(ch_dev, frames_dev + taps // HOP - 1, HOP)
    banded = filters.reshape(taps, groups, GW)
    total = jnp.zeros((ch_dev, groups, frames_dev, GW), jnp.float32)
    for k in range(taps // HOP):
        total = total + jnp.einsum(
            "cfh,hgw->cgfw",
            blocks[:, k : k + frames_dev],
            banded[k * HOP : (k + 1) * HOP],
            preferred_element_type=jnp.float32,
        )
    features = total.astype(jnp.bfloat16).reshape(ch_dev, groups, frames_dev * GW)
    tm_count = lax.axis_size("tm")
    fiber_count = lax.axis_size("fiber")
    rows = ch_dev * fiber_count // tm_count
    local_groups = groups // fiber_count
    by_band = lax.all_to_all(features, "fiber", split_axis=1, concat_axis=0, tiled=True)
    owned = lax.all_to_all(by_band, "tm", split_axis=0, concat_axis=2, tiled=True)
    framed = extended_2(owned, (("tm", 0),), 1)
    frames = framed.shape[2] // GW
    planes = framed.reshape(rows + 2, local_groups, frames, GW).transpose(0, 1, 3, 2)
    planes = jnp.pad(planes, ((0, 0), (0, 0), (0, 0), (1, 1)))
    start_row = lax.axis_index("tm") * rows
    edge = jnp.array([-1], jnp.int32)
    sec_all = jnp.concatenate([edge, channel_section, edge])
    sec = lax.dynamic_slice_in_dim(sec_all, start_row, rows + 2, 0)
    same_lo = (sec[:-2] == sec[1:-1]).astype(jnp.bfloat16)
    same_hi = (sec[2:] == sec[1:-1]).astype(jnp.bfloat16)
    middle_sec = sec[1:-1]
    table = lax.dynamic_slice_in_dim(
        section_bank, lax.axis_index("fiber") * local_groups, local_groups, 1
    )
    onehot = (middle_sec[:, None] == jnp.arange(table.shape[0], dtype=jnp.int32)[None, :]).astype(
        jnp.int32
    )
    choose = jnp.dot(onehot, table)
    banks = conv_bank.shape[0]
    pick_all = (choose[:, :, None] == jnp.arange(banks, dtype=jnp.int32)[None, None, :]).astype(
        jnp.float32
    )
    block = math.gcd(rows, 32)
    count = rows // block

    def conv_rows(start):
        xs = lax.dynamic_slice_in_dim(planes, start, block + 2, 0)
        low = lax.dynamic_slice_in_dim(same_lo, start, block, 0)
        high = lax.dynamic_slice_in_dim(same_hi, start, block, 0)
        pick = lax.dynamic_slice_in_dim(pick_all, start, block, 0)
        acc = jnp.zeros((block, local_groups, banks, GW, frames), jnp.float32)
        for d in range(3):
            part = xs[d : d + block]
            if d == 0:
                part = part * low[:, None, None, None]
            if d == 2:
                part = part * high[:, None, None, None]
            for e in range(3):
                acc = acc + jnp.einsum(
                    "bgoi,cgit->cgbot",
                    conv_bank[:, :, d, e],
                    part[..., e : e + frames],
                    preferred_element_type=jnp.float32,
                )
        out = jnp.sum(acc * pick[:, :, :, None, None], axis=2)
        return out.astype(jnp.bfloat16).reshape(block, local_groups * GW, frames)

    starts = jnp.arange(count, dtype=jnp.int32) * block
    result = lax.map(conv_rows, starts)
    return result.reshape(rows, local_groups * GW, frames)


def solution(mesh):
    placed = (P("fiber", "tm"), P(), P(), P(), P(None, "fiber", None, None, None, None))
    return jax.shard_map(
        shards, mesh=mesh, in_specs=placed, out_specs=P("tm", "fiber", None), check_vma=False
    )
```

profile of v0, /device:TPU:16, one launch (start us, length us, event | category | flops | bytes accessed | tf_op | source)
XLA Modules:
  0.0 503.0 jit_solution(869214238077134214)
XLA Ops:
  0.0 2.9 copy.33
  3.0 7.5 %collective-permute-start = (bf16[512,384]{0,1:T(8,128)(2,1)S(1)}, bf16[512,384]{0,1:T(8,128)(2,1)S(1)}, u32[]{:S(2)}, u32[]{:S(2)}) collective-permute-start(bf16[512,384]{0,1:T(8,128)(2,1)S(1)} %slice.152), channel_id=1, source_target_pairs={{8,0},{16,8},{24,16},{32,24},{40,32},{48,40},{56,48},{64,56},{72,6... | collective-permute-start | bytes 1179656 | tf_op jit(solution)/shard_map/ppermute | solution.py:15
  11.0 9.0 %collective-permute-done = bf16[512,384]{0,1:T(8,128)(2,1)S(1)} collective-permute-done((bf16[512,384]{0,1:T(8,128)(2,1)S(1)}, bf16[512,384]{0,1:T(8,128)(2,1)S(1)}, u32[]{:S(2)}, u32[]{:S(2)}) %collective-permute-start) | collective-permute-done | bytes 393248 | tf_op jit(solution)/shard_map/ppermute | solution.py:15
  21.5 4.5 fusion.33
  26.0 4.5 fusion.34
  30.6 8.7 %fusion.31 = bf16[512,8,16,32]{0,3,1,2:T(8,128)(2,1)} fusion(f32[512,16,8,32]{0,3,2,1:T(8,128)S(1)} %fusion.32, f32[512,16,8,32]{0,3,2,1:T(8,128)} %fusion.34, f32[512,16,8,32]{0,3,2,1:T(8,128)} %fusion.33, bf16[128,8,32,1]{0,2,1,3:T(8,128)(2,1)S(1)} %bitcast.227, bf16[512,19,128]{0,2,1:T(8,128)(2,1)S(1)} %bitcast.217), kind=kOutput, calls=%fused_computation.47 | convolution fusion | flops 545259520 | bytes 31522816 | tf_op jit(solution)/shard_map/cfh,hgw->cgfw/dot_general | solution.py:42
  39.3 2.7 copy.42
  42.0 51.7 %all_to_all.33 = bf16[512,8,512]{0,2,1:T(8,128)(2,1)} all-to-all(bf16[512,8,512]{0,2,1:T(8,128)(2,1)S(1)} %bitcast.222), channel_id=1, replica_groups=mesh['tm'=32,'fiber'=8] {'fiber'}, dimensions={1} | all-to-all | bytes 8388608 | tf_op jit(solution)/shard_map/all_to_all | solution.py:53
  93.6 6.4 %copy.43 = bf16[8,512,1,512]{3,1,0,2:T(8,128)(2,1)} copy(bf16[8,512,1,512]{1,3,0,2:T(8,128)(2,1)} %bitcast.223) | data formatting | bytes 8388608 | tf_op jit(solution)/shard_map/all_to_all | solution.py:53
  100.7 6.7 %reduce.5 = bf16[4096,512]{1,0:T(8,128)(2,1)} reduce(bf16[4096,1,512]{2,0,1:T(8,128)(2,1)} %bitcast.221, bf16[]{:T(256)} %broadcast.38), dimensions={1}, to_apply=%copy.44.reduce_sub_computation | reduce | bytes 8388610 | tf_op jit(solution)/shard_map/all_to_all | solution.py:53
  107.3 7.8 %reshape.199 = bf16[32,2,32768]{2,1,0:T(2,128)(2,1)} reshape(bf16[4096,512]{1,0:T(8,128)(2,1)} %reduce.5) | data formatting | bytes 8388608
  115.1 9.6 %all-to-all-start.1 = ((bf16[32,2,32768]{2,1,0:T(2,128)(2,1)}), bf16[32,2,32768]{2,1,0:T(2,128)(2,1)}, u32[]{:S(2)}, u32[]{:S(2)}) async-start(bf16[32,2,32768]{2,1,0:T(2,128)(2,1)} %reshape.199), calls=%async_computation.1 | async-start | bytes 8388608 | tf_op jit(solution)/shard_map/all_to_all | solution.py:54
  125.3 95.0 %all-to-all-done.1 = bf16[32,2,32768]{2,1,0:T(2,128)(2,1)} async-done(((bf16[32,2,32768]{2,1,0:T(2,128)(2,1)}), bf16[32,2,32768]{2,1,0:T(2,128)(2,1)}, u32[]{:S(2)}, u32[]{:S(2)}) %all-to-all-start.1) | async-done | bytes 4194336 | tf_op jit(solution)/shard_map/all_to_all | solution.py:54
  220.2 19.8 %reshape.200 = bf16[4096,1,512]{2,1,0:T(2,128)(2,1)} reshape(bf16[32,2,32768]{2,1,0:T(2,128)(2,1)} %all-to-all-done.1) | data formatting | bytes 8388608
  240.1 4.7 copy.63
  244.7 1.9 copy-done.2
  248.7 6.8 %collective-permute-start.2 = (bf16[1,1,16384]{2,1,0:T(2,128)(2,1)S(1)}, bf16[1,1,16384]{2,1,0:T(2,128)(2,1)S(1)}, u32[]{:S(2)}, u32[]{:S(2)}) collective-permute-start(bf16[1,1,16384]{2,1,0:T(2,128)(2,1)S(1)} %bitcast.228), channel_id=1, source_target_pairs={{8,0},{16,8},{24,16},{32,24},{40,32},{48,40},{56,48},{64,56},{72,6... | collective-permute-start | bytes 98312 | tf_op jit(solution)/shard_map/ppermute | solution.py:26
  255.6 6.5 %copy.45 = bf16[128,1,32,512]{0,3,2,1:T(8,128)(2,1)} copy(bf16[128,1,32,512]{3,0,2,1:T(8,128)(2,1)} %bitcast.219) | data formatting | bytes 8388608 | tf_op jit(solution)/shard_map/all_to_all | solution.py:54
  262.3 9.5 %concatenate.22 = bf16[1,1,512,32]{0,3,2,1:T(8,128)(2,1)} reshape(bf16[16384]{0:T(1024)(128)(2,1)S(1)} %reduce.2) | data formatting | bytes 65536 | tf_op jit(solution)/shard_map/concatenate | solution.py:27
  272.0 9.5 %concatenate.23 = bf16[1,1,512,32]{0,3,2,1:T(8,128)(2,1)} reshape(bf16[16384]{0:T(1024)(128)(2,1)S(1)} %reduce.3) | data formatting | bytes 65536 | tf_op jit(solution)/shard_map/concatenate | solution.py:27
  281.5 10.6 %maximum_bitcast_fusion = bf16[130,1,32,512]{0,2,3,1:T(8,128)(2,1)} fusion(bf16[1,1,512,32]{0,3,2,1:T(8,128)(2,1)} %concatenate.23, bf16[128,1,512,32]{0,3,2,1:T(8,128)(2,1)} %bitcast.220, bf16[1,1,512,32]{0,3,2,1:T(8,128)(2,1)} %concatenate.22), kind=kLoop, calls=%fused_computation.45 | loop fusion | flops 12779520 | bytes 8519680 | tf_op jit(solution)/shard_map/transpose | solution.py:57
  292.1 14.6 %copy.68 = bf16[130,1,32,512]{3,2,0,1:T(8,128)(2,1)} copy(bf16[130,1,32,512]{0,2,3,1:T(8,128)(2,1)} %maximum_bitcast_fusion) | data formatting | bytes 8519680
  306.7 7.3 %pad.4.clone = bf16[130,1,32,514]{3,2,0,1:T(8,128)(2,1)} pad(bf16[130,1,32,512]{3,2,0,1:T(8,128)(2,1)} %copy.68, bf16[]{:T(256)} %constant.11.clone.1), padding=0_0x0_0x0_0x1_1 | pad | bytes 8536322 | tf_op jit(solution)/shard_map/jit(_pad)/pad | solution.py:58
  314.0 188.3 %while.10 = (s32[]{:T(128)}, bf16[4,32,32,512]{3,2,1,0:T(8,128)(2,1)}, s32[4]{0:T(128)S(1)}, bf16[130,1,32,514]{3,2,0,1:T(8,128)(2,1)}, bf16[128]{0:T(256)(128)(...) while((s32[]{:T(128)}, ...), condition=%wide.region_2.3_spmd, body=%wide.region_0.2_spmd.sunk | while | flops 614993920 | bytes 84068520 | solution.py:103
  317.6 2.1 dynamic-slice_multiply_fusion.3
  319.7 2.9 fusion.72
  322.6 2.9 fusion.73
  325.4 2.9 fusion.77
  328.4 2.8 fusion.78
  331.1 2.9 fusion.79
  334.0 4.1 fusion.74
  338.1 4.2 fusion.75
  342.3 4.1 fusion.76
  346.6 13.5 %fusion.81 = bf16[32,512,32]{1,2,0:T(8,128)(2,1)S(1)} fusion(f32[32,512,2,32]{1,3,2,0:T(8,128)} %fusion.72, f32[32,512,2,32]{1,3,2,0:T(8,128)} %fusion.73, f32[32,512,2,32]{1,3,2,0:T(8,128)} %fusion.74, f32[32,512,2,32]{1,3,2,0:T(8,128)} %fusion.75, f32[32,512,2,32]{1,3,2,0:T(8,128)} %fusion.76, f32[32,512,2,32]{1,3,2,0:T(8,128)} %fusion.77, ...), kind=kOutput, calls=%fused_computation.1.clone.1 | convolution fusion | flops 77070336 | bytes 35684352 | tf_op jit(solution)/shard_map/while/body/eval_jaxpr/bgoi,cgit->cgbot/dot_general | solution.py:93
  364.7 2.0 dynamic-slice_multiply_fusion.3
  366.8 2.9 fusion.72
  369.6 2.9 fusion.73
  372.5 2.9 fusion.77
  375.4 2.7 fusion.78
  378.2 2.9 fusion.79
  381.1 4.1 fusion.74
  385.2 4.2 fusion.75
  389.4 4.1 fusion.76
  393.6 13.5 %fusion.81 = bf16[32,512,32]{1,2,0:T(8,128)(2,1)S(1)} fusion(f32[32,512,2,32]{1,3,2,0:T(8,128)} %fusion.72, f32[32,512,2,32]{1,3,2,0:T(8,128)} %fusion.73, f32[32,512,2,32]{1,3,2,0:T(8,128)} %fusion.74, f32[32,512,2,32]{1,3,2,0:T(8,128)} %fusion.75, f32[32,512,2,32]{1,3,2,0:T(8,128)} %fusion.76, f32[32,512,2,32]{1,3,2,0:T(8,128)} %fusion.77, ...), kind=kOutput, calls=%fused_computation.1.clone.1 | convolution fusion | flops 77070336 | bytes 35684352 | tf_op jit(solution)/shard_map/while/body/eval_jaxpr/bgoi,cgit->cgbot/dot_general | solution.py:93
  411.8 2.0 dynamic-slice_multiply_fusion.3
  413.8 2.9 fusion.72
  416.7 2.9 fusion.73
  419.6 2.9 fusion.77
  422.5 2.7 fusion.78
  425.2 2.9 fusion.79
  428.1 4.1 fusion.74
  432.3 4.2 fusion.75
  436.5 4.1 fusion.76
  440.7 13.5 %fusion.81 = bf16[32,512,32]{1,2,0:T(8,128)(2,1)S(1)} fusion(f32[32,512,2,32]{1,3,2,0:T(8,128)} %fusion.72, f32[32,512,2,32]{1,3,2,0:T(8,128)} %fusion.73, f32[32,512,2,32]{1,3,2,0:T(8,128)} %fusion.74, f32[32,512,2,32]{1,3,2,0:T(8,128)} %fusion.75, f32[32,512,2,32]{1,3,2,0:T(8,128)} %fusion.76, f32[32,512,2,32]{1,3,2,0:T(8,128)} %fusion.77, ...), kind=kOutput, calls=%fused_computation.1.clone.1 | convolution fusion | flops 77070336 | bytes 35684352 | tf_op jit(solution)/shard_map/while/body/eval_jaxpr/bgoi,cgit->cgbot/dot_general | solution.py:93
  458.9 2.0 dynamic-slice_multiply_fusion.3
  460.9 2.9 fusion.72
  463.7 2.9 fusion.73
  466.6 2.9 fusion.77
  469.5 2.7 fusion.78
  472.3 2.9 fusion.79
  475.2 4.1 fusion.74
  479.3 4.2 fusion.75
  483.5 4.1 fusion.76
  487.7 13.5 %fusion.81 = bf16[32,512,32]{1,2,0:T(8,128)(2,1)S(1)} fusion(f32[32,512,2,32]{1,3,2,0:T(8,128)} %fusion.72, f32[32,512,2,32]{1,3,2,0:T(8,128)} %fusion.73, f32[32,512,2,32]{1,3,2,0:T(8,128)} %fusion.74, f32[32,512,2,32]{1,3,2,0:T(8,128)} %fusion.75, f32[32,512,2,32]{1,3,2,0:T(8,128)} %fusion.76, f32[32,512,2,32]{1,3,2,0:T(8,128)} %fusion.77, ...), kind=kOutput, calls=%fused_computation.1.clone.1 | convolution fusion | flops 77070336 | bytes 35684352 | tf_op jit(solution)/shard_map/while/body/eval_jaxpr/bgoi,cgit->cgbot/dot_general | solution.py:93
  (59 shorter events, 14.0 us)
Async XLA Ops:
  0.0 125.0 %copy-start = (s32[128,8]{0,1:T(8,128)S(1)}, s32[128,8]{0,1:T(8,128)}, u32[]{:S(2)}) copy-start(s32[128,8]{0,1:T(8,128)} %param.11) | copy-start | bytes 12292
  0.0 10.5 %copy-start.3 = (bf16[512,256]{1,0:T(8,128)(2,1)S(1)}, bf16[512,256]{1,0:T(8,128)(2,1)}, u32[]{:S(2)}) copy-start(bf16[512,256]{1,0:T(8,128)(2,1)} %param.9) | copy-start | bytes 786436
  3.0 17.1 %collective-permute-start = (bf16[512,384]{0,1:T(8,128)(2,1)S(1)}, bf16[512,384]{0,1:T(8,128)(2,1)S(1)}, u32[]{:S(2)}, u32[]{:S(2)}) collective-permute-start(bf16[512,384]{0,1:T(8,128)(2,1)S(1)} %slice.152), channel_id=1, source_target_pairs={{8,0},{16,8},{24,16},{32,24},{40,32},{48,40},{56,48},{64,56},{72,6... | collective-permute-start | bytes 1179656 | tf_op jit(solution)/shard_map/ppermute | solution.py:15
  115.1 9.6 %copy-start.5 = (s32[4096]{0:T(1024)S(1)}, s32[4096]{0:T(1024)}, u32[]{:S(2)}) copy-start(s32[4096]{0:T(1024)} %param.10) | copy-start | bytes 49156
  115.1 105.1 %all-to-all-start.1 = ((bf16[32,2,32768]{2,1,0:T(2,128)(2,1)}), bf16[32,2,32768]{2,1,0:T(2,128)(2,1)}, u32[]{:S(2)}, u32[]{:S(2)}) async-start(bf16[32,2,32768]{2,1,0:T(2,128)(2,1)} %reshape.199), calls=%async_computation.1 | async-start | bytes 8388608 | tf_op jit(solution)/shard_map/all_to_all | solution.py:54
  240.0 15.5 %copy-start.4 = (bf16[2,1,3,3,32,32]{5,4,3,2,1,0:T(8,128)(2,1)S(1)}, bf16[2,1,3,3,32,32]{5,4,3,2,1,0:T(8,128)(2,1)}, u32[]{:S(2)}) copy-start(bf16[2,1,3,3,32,32]{5,4,3,2,1,0:T(8,128)(2,1)} %param.12) | copy-start | bytes 110596
  244.7 1.9 copy-start.2
  246.8 15.3 %collective-permute-start.1 = (bf16[1,1,16384]{2,1,0:T(2,128)(2,1)S(1)}, bf16[1,1,16384]{2,1,0:T(2,128)(2,1)S(1)}, u32[]{:S(2)}, u32[]{:S(2)}) collective-permute-start(bf16[1,1,16384]{2,1,0:T(2,128)(2,1)S(1)} %bitcast.229), channel_id=1, source_target_pairs={{0,8},{8,16},{16,24},{24,32},{32,40},{40,48},{48,56},{56,64},{64,7... | collective-permute-start | bytes 98312 | tf_op jit(solution)/shard_map/ppermute | solution.py:25
  248.7 23.1 %collective-permute-start.2 = (bf16[1,1,16384]{2,1,0:T(2,128)(2,1)S(1)}, bf16[1,1,16384]{2,1,0:T(2,128)(2,1)S(1)}, u32[]{:S(2)}, u32[]{:S(2)}) collective-permute-start(bf16[1,1,16384]{2,1,0:T(2,128)(2,1)S(1)} %bitcast.228), channel_id=1, source_target_pairs={{8,0},{16,8},{24,16},{32,24},{40,32},{48,40},{56,48},{64,56},{72,6... | collective-permute-start | bytes 98312 | tf_op jit(solution)/shard_map/ppermute | solution.py:26
  502.3 0.7 copy-start.1
where the time goes:
time: 505 us; the launch traced here: 503 us
  matrix products  180 us (36%)
  local copies, waits for them, and re-layouts  104 us (21%)
  waiting for transfers between devices  104 us (21%)
  blocking collectives  51.7 us (10%)
  other arithmetic  26.1 us (5%)
  starting transfers between devices  25.9 us (5%)
  loops' own time  11.6 us (2%)
    dot_general x36, matrix products, conv_rows(): jnp.einsum('bgoi,cgit->cgbot', conv_bank[:, :, d, e], part[..., e:e + fra...  161 us
    all_to_all x1, waiting for transfers between devices, shards(): lax.all_to_all(by_band, 'tm', split_axis=0, concat_axis=2, tiled=True)  95 us
    unnamed x17, local copies, waits for them, and re-layouts  52.4 us
    all_to_all x1, blocking collectives, shards(): lax.all_to_all(features, 'fiber', split_axis=1, concat_axis=0, tiled=True)  51.7 us
    dot_general x4, matrix products, shards(): jnp.einsum('cfh,hgw->cgfw', blocks[:, k:k + frames_dev], banded[k * HOP:(...  19.1 us
    concatenate x2, local copies, waits for them, and re-layouts, extended_2(): x = jnp.concatenate([before, x, after], axis=dim)  19.1 us
    another operation x1, loops' own time, shards(): result = lax.map(conv_rows, starts)  11.6 us
    transpose x1, other arithmetic, shards(): framed.reshape(rows + 2, local_groups, frames, GW).transpose(0, 1, 3, 2)  10.6 us
  transfers between devices with their start and end apart: 4, of which 2 were waited for; matrix products, arithmetic and copies ran while one was open for 3% of the time, Pallas kernels for 0%

commit v1 on v0

v1 whole, which is shorter than its diff:
```python
import jax
import jax.numpy as jnp
from jax import lax
from jax.experimental import pallas as pl
from jax.experimental.pallas import tpu as pltpu
from jax.sharding import PartitionSpec as P

HOP = 128
GW = 32
AXES = ("tm", "fiber")


PLACES = [(x, y, z, c) for x in range(4) for y in range(4) for z in range(8) for c in range(2)]


def flat(x, y, z, c):
    return ((y * 4 + z // 2) * 2 + c) * 8 + x * 2 + z % 2


def spot(x, y, late, odd, b, core, early):
    nx = (x - y + 2 * b + core - early) % 4
    return flat(nx, x, 4 * odd + 2 * b + (late ^ odd), core)


def bulk_route(step, swap):
    pairs = []
    for x, y, z, c in PLACES:
        pair, odd = z // 2, z % 2
        late = 0 if pair in (0, 3) else 1
        b = step ^ (pair // 2)
        pairs.append((flat(x, y, z, c), spot(x, y, late, odd, b, c ^ swap, int(pair == 3))))
    return pairs


def rim_route(b, core):
    return [
        (flat(x, y, z, c), spot(x, y, int(z // 2 == 3), z % 2, b, core, 0))
        for x, y, z, c in PLACES
        if c == 0 and z // 2 in (1, 3)
    ]


def filter_kernel(where_ref, *refs):
    pieces, rims, (taps_ref, out_ref, seq_ref) = refs[:4], refs[4:8], refs[8:]
    first, core, keep = where_ref[0], where_ref[1], where_ref[2]
    chans = seq_ref.shape[0]

    @pl.loop(0, pieces[0].shape[0] // chans)
    def _(i):
        rows = pl.ds(i * chans, chans)
        for j, ref in enumerate(pieces):
            at = (first ^ (j >> 1)) * 48 + (core ^ (j & 1)) * 16
            seq_ref[:, pl.ds(pl.multiple_of(at, 16), 16), :] = ref[rows]
        seq_ref[:, 32:48, :] = seq_ref[:, 48:64, :] * keep.astype(jnp.bfloat16)
        seq_ref[:, 80:83, :] = (rims[0][rows] + rims[1][rows]) + (rims[2][rows] + rims[3][rows])
        columns = []
        for k in range(4):
            runs = [seq_ref[:, s + k : s + k + 32, :] for s in (0, 48)]
            columns.append(jnp.concatenate(runs, axis=1).reshape(chans * 64, HOP))
        frames = jnp.concatenate(columns, axis=1)
        feats = lax.dot_general(
            taps_ref[...], frames, (((1,), (1,)), ((), ())), preferred_element_type=jnp.float32
        ).astype(jnp.bfloat16)
        for g in range(8):
            for p in range(chans // 2):
                out_ref[g, i * (chans // 2) + p] = feats[
                    g * GW : (g + 1) * GW, p * 128 : (p + 1) * 128
                ]


def weight_kernel(flag_ref, kern_ref, out_ref, base_ref):
    block = pl.program_id(0)

    @pl.when(block == 0)
    def _():
        r = lax.broadcasted_iota(jnp.int32, (288, 960), 0)
        k = lax.broadcasted_iota(jnp.int32, (288, 960), 1)
        lag = k - r - 224 * ((r >= 96).astype(jnp.int32) + (r >= 192).astype(jnp.int32))
        for c in range(8):
            spread = jnp.where(lag == 32 * c, 1.0, 0.0).astype(jnp.bfloat16)
            base_ref[c] = jnp.dot(kern_ref[...], spread, preferred_element_type=jnp.float32)

    k = lax.broadcasted_iota(jnp.int32, (1, 960), 1)
    k = k - 320 * ((k >= 320).astype(jnp.int32) + (k >= 640).astype(jnp.int32))
    for c in range(8):
        at = block * 8 + c
        low, high = flag_ref[1, at].astype(jnp.float32), flag_ref[2, at].astype(jnp.float32)
        mask = jnp.where(k < 32 * c + 32, low, jnp.where(k >= 32 * c + 64, high, 1.0))
        rows = base_ref[c, pl.ds(pl.multiple_of(flag_ref[0, at] * GW, GW), GW), :]
        out_ref[0, c * GW : (c + 1) * GW, :] = (rows * mask).astype(jnp.bfloat16)


def assemble(x_ref, load, pairs, sides, place):
    size = pairs * GW
    lane = lax.broadcasted_iota(jnp.int16, (size, 128), 1)
    v = [load(q).reshape(size, 128) for q in range(8)]
    near = [pltpu.roll(u, 32, 1) for u in v]
    far = [pltpu.roll(u, 96, 1) for u in v]
    zero = jnp.zeros((size, 128), jnp.bfloat16)
    for side in sides:
        outer, inner = (near, far) if side else (far, near)
        t = [
            jnp.where(
                lane < 32,
                outer[2 * m],
                jnp.where(lane < 96, inner[2 * m + 1], outer[(2 * m + 2) % 8]),
            )
            for m in range(4)
        ]
        back = [pltpu.roll(u, 1, 1) for u in t]
        ahead = [pltpu.roll(u, 127, 1) for u in t]
        for m in range(4):
            before = jnp.where(lane == 0, back[m - 1] if m else zero, back[m])
            after = jnp.where(lane == 127, ahead[m + 1] if m < 3 else zero, ahead[m])
            for e, u in enumerate((before, t[m], after)):
                for p in range(pairs):
                    x_ref[e, place(p, side), :, m * 128 : (m + 1) * 128] = u[
                        p * GW : (p + 1) * GW
                    ]


def conv_kernel(slot_ref, recv_ref, w_ref, out_ref, x_ref):
    step = pl.program_id(0)

    def group(g):
        assemble(
            x_ref,
            lambda q: recv_ref[slot_ref[q], pl.ds(g * 4, 4)],
            4,
            (0, 1),
            lambda p, side: 8 * g + 1 + 2 * p + side,
        )

    def multiply():
        x = jnp.concatenate(
            [x_ref[e, pl.ds(8 * step, 10)].reshape(10 * GW, 512) for e in range(3)], axis=0
        )
        res = jnp.dot(w_ref[0], x, preferred_element_type=jnp.float32)
        out_ref[...] = res.astype(jnp.bfloat16).reshape(8, GW, 512)

    @pl.when(step == 0)
    def _():
        assemble(x_ref, lambda q: recv_ref[slot_ref[q], 64], 1, (0, 1), lambda p, side: 129 * side)
        group(0)

    @pl.when(step < 15)
    def _():
        group(step + 1)
        multiply()

    @pl.when(step == 15)
    def _():
        multiply()


def whole(*shape):
    return pl.BlockSpec(shape, lambda i, s: (0,) * len(shape))


def shards(waveform, filters, channel_section, section_bank, conv_bank):
    tm, fiber = lax.axis_index("tm"), lax.axis_index("fiber")
    y, zh, core, x, z0 = tm >> 3, (tm >> 1) & 3, tm & 1, fiber >> 1, fiber & 1
    z2, z1 = zh >> 1, zh & 1
    late = z0 ^ z2
    first = 1 ^ z1 ^ late
    turn = 2 * z1 + core
    vmem = pl.BlockSpec(memory_space=pltpu.VMEM)

    up = [(i, i + 1) for i in range(7)]
    row_low = lax.ppermute(waveform[511:], "fiber", up)
    row_high = lax.ppermute(waveform[:1], "fiber", [(j, i) for i, j in up])
    edge_rows = jnp.concatenate(
        [row_low]
        + [waveform[i : i + 1] for i in (128, 127, 256, 255, 384, 383)]
        + [row_high],
        axis=0,
    ).reshape(4, 2, 2048)

    def block_rows(at):
        main = lax.dynamic_slice_in_dim(waveform, 128 * at, 128, 0)
        sides = lax.dynamic_index_in_dim(edge_rows, at, 0, False)
        return main.reshape(128, 16, HOP), sides.reshape(2, 16, HOP)

    pieces, rims = [], []
    for step in (0, 1):
        for swap in (0, 1):
            part = jnp.concatenate(block_rows(2 * (step ^ z2) + (core ^ swap)), axis=0)
            pieces.append(lax.ppermute(part, AXES, bulk_route(step, swap)))
    for b in (0, 1):
        for c in (0, 1):
            part = jnp.concatenate(
                [
                    waveform[128 * (2 * b + c) : 128 * (2 * b + c + 1), : 3 * HOP],
                    edge_rows[2 * b + c, :, : 3 * HOP],
                ],
                axis=0,
            ).reshape(130, 3, HOP)
            rims.append(lax.ppermute(part, AXES, rim_route(b, c)))

    edge = jnp.array([-1], jnp.int32)
    sec = lax.dynamic_slice_in_dim(
        jnp.concatenate([edge, channel_section, edge]), tm * 128, 130, 0
    )
    middle = sec[1:-1]
    table = lax.dynamic_slice_in_dim(section_bank, fiber, 1, 1)
    onehot = (middle[:, None] == jnp.arange(table.shape[0], dtype=jnp.int32)[None, :]).astype(
        jnp.int32
    )
    choose = jnp.sum(onehot * table[:, 0][None, :], axis=1)
    flags = jnp.stack([choose, sec[:-2] == middle, sec[2:] == middle]).astype(jnp.int32)
    kern = conv_bank[:, 0].transpose(0, 3, 2, 1, 4).reshape(64, 288)
    weights = pl.pallas_call(
        weight_kernel,
        out_shape=jax.ShapeDtypeStruct((16, 256, 960), jnp.bfloat16),
        grid_spec=pltpu.PrefetchScalarGridSpec(
            num_scalar_prefetch=1,
            grid=(16,),
            in_specs=[whole(64, 288)],
            out_specs=pl.BlockSpec((1, 256, 960), lambda i, s: (i, 0, 0)),
            scratch_shapes=[pltpu.VMEM((8, 64, 960), jnp.float32)],
        ),
        cost_estimate=pl.CostEstimate(
            flops=8 * 2 * 64 * 288 * 960, bytes_accessed=8 << 20, transcendentals=0
        ),
        name="weights",
    )(flags, kern)

    keep = jnp.where((late == 0) & (((y - x + turn) & 3) == 0), 0, 1)
    where = jnp.stack([first, core, keep]).astype(jnp.int32)
    feats = pl.pallas_call(
        filter_kernel,
        out_shape=jax.ShapeDtypeStruct((8, 65, GW, 128), jnp.bfloat16),
        in_specs=[pl.BlockSpec(memory_space=pltpu.SMEM)] + [vmem] * 9,
        out_specs=vmem,
        scratch_shapes=[pltpu.VMEM((26, 96, HOP), jnp.bfloat16)],
        cost_estimate=pl.CostEstimate(
            flops=2 * 8320 * 512 * 256, bytes_accessed=6 << 20, transcendentals=0
        ),
        name="filterbank",
    )(where, *pieces, *rims, filters.T)
    recv = lax.all_to_all(feats, "fiber", 0, 0, tiled=True)

    q = jnp.arange(8, dtype=jnp.int32)
    slot = (2 * ((y + turn - (q >> 1)) & 3) + ((q & 1) ^ z2)).astype(jnp.int32)
    return pl.pallas_call(
        conv_kernel,
        out_shape=jax.ShapeDtypeStruct((128, GW, 512), jnp.bfloat16),
        grid_spec=pltpu.PrefetchScalarGridSpec(
            num_scalar_prefetch=1,
            grid=(16,),
            in_specs=[vmem, pl.BlockSpec((1, 256, 960), lambda i, s: (i, 0, 0))],
            out_specs=pl.BlockSpec((8, GW, 512), lambda i, s: (i, 0, 0)),
            scratch_shapes=[pltpu.VMEM((3, 130, GW, 512), jnp.bfloat16)],
        ),
        cost_estimate=pl.CostEstimate(
            flops=16 * 2 * 256 * 960 * 512, bytes_accessed=16 << 20, transcendentals=0
        ),
        name="conv",
    )(slot, recv, weights)


def solution(mesh):
    placed = (P("fiber", "tm"), P(), P(), P(), P(None, "fiber", None, None, None, None))

    return jax.shard_map(
        shards, mesh=mesh, in_specs=placed, out_specs=P("tm", "fiber", None), check_vma=False
    )
```

time: 505 us -> 187 us (0.37)
  the two profiles are of different devices: /device:TPU:16 before, /device:TPU:92 now
where the time goes in v1:
time: 187 us
  waiting for transfers between devices  72.7 us (39%)
  starting transfers between devices  67 us (36%)
  Pallas kernels  34.6 us (19%)
  local copies, waits for them, and re-layouts  9.27 us (5%)
  other arithmetic  2.6 us (1%)
    all_to_all x1, starting transfers between devices, shards(): recv = lax.all_to_all(feats, 'fiber', 0, 0, tiled=True)  39.6 us
    all_to_all x1, waiting for transfers between devices, shards(): recv = lax.all_to_all(feats, 'fiber', 0, 0, tiled=True)  38.3 us
    ppermute x4, waiting for transfers between devices, shards(): rims.append(lax.ppermute(part, AXES, rim_route(b, c)))  34.4 us
    pallas_call x1, Pallas kernels, shards(): pl.pallas_call(conv_kernel, out_shape=jax.ShapeDtypeStruct((128, GW, 512)...  17.6 us
    ppermute x4, starting transfers between devices, shards(): rims.append(lax.ppermute(part, AXES, rim_route(b, c)))  11.7 us
    ppermute x4, starting transfers between devices, shards(): pieces.append(lax.ppermute(part, AXES, bulk_route(step, swap)))  9.88 us
    pallas_call x1, Pallas kernels, shards(): pl.pallas_call(weight_kernel, out_shape=jax.ShapeDtypeStruct((16, 256, 96...  9.49 us
    pallas_call x1, Pallas kernels, shards(): pl.pallas_call(filter_kernel, out_shape=jax.ShapeDtypeStruct((8, 65, GW,...  7.57 us
  transfers between devices with their start and end apart: 11, of which 5 were waited for; matrix products, arithmetic and copies ran while one was open for 5% of the time, Pallas kernels for 5%

profile of v1, /device:TPU:92, one launch (start us, length us, event | category | flops | bytes accessed | tf_op | source)
XLA Modules:
  0.0 186.6 jit_solution(10270953713626107815)
XLA Ops:
  0.0 1.0 fusion.4
  1.0 3.8 %collective-permute-start.1 = (bf16[1,2048]{1,0:T(2,128)(2,1)S(1)}, bf16[1,2048]{1,0:T(2,128)(2,1)S(1)}, u32[]{:S(2)}, u32[]{:S(2)}) collective-permute-start(bf16[1,2048]{1,0:T(2,128)(2,1)S(1)} %get-tuple-element.13), channel_id=1, source_target_pairs={{1,0},{2,1},{3,2},{4,3},{5,4},{6,5},{7,6},{9,8},{10,9},{11,10},{12... | collective-permute-start | bytes 12296 | tf_op jit(solution)/shard_map/ppermute | solution.py:171
  4.8 2.0 %collective-permute-start = (bf16[1,2048]{1,0:T(2,128)(2,1)S(1)}, bf16[1,2048]{1,0:T(2,128)(2,1)S(1)}, u32[]{:S(2)}, u32[]{:S(2)}) collective-permute-start(bf16[1,2048]{1,0:T(2,128)(2,1)S(1)} %get-tuple-element.20), channel_id=1, source_target_pairs={{0,1},{1,2},{2,3},{3,4},{4,5},{5,6},{6,7},{8,9},{9,10},{10,11},{11... | collective-permute-start | bytes 12296 | tf_op jit(solution)/shard_map/ppermute | solution.py:170
  6.9 1.1 fusion.3
  8.0 1.7 dynamic-slice_bitcast_fusion
  9.7 0.9 copy.28
  10.6 0.1 copy.36
  10.7 0.1 copy.27
  10.8 0.1 copy.35
  11.0 0.1 copy.25
  11.1 0.1 copy.34
  11.2 0.1 copy.23
  11.4 0.1 copy.33
  11.5 0.1 copy.21
  11.7 0.1 copy.43
  11.8 0.1 copy.41
  11.9 0.1 copy.39
  12.0 0.1 copy.37
  12.2 0.0 collective-permute-done.1
  12.2 0.0 collective-permute-done
  12.2 0.1 concatenate.50
  12.5 0.1 pad_maximum_fusion
  12.6 1.9 %collective-permute-start.2 = (bf16[130,16,128]{2,1,0:T(8,128)(2,1)S(1)}, bf16[130,16,128]{2,1,0:T(8,128)(2,1)S(1)}, u32[]{:S(2)}, u32[]{:S(2)}) collective-permute-start(bf16[130,16,128]{2,1,0:T(8,128)(2,1)S(1)} %pad_maximum_fusion), channel_id=1, source_target_pairs={{0,0},{8,10},{1,33},{9,43},{16,1},{24,11},{17,32},{25,42},{32,21},... | collective-permute-start | bytes 1597448 | tf_op jit(solution)/shard_map/ppermute | solution.py:188
  14.6 5.8 %collective-permute-start.3 = (bf16[130,16,128]{2,1,0:T(8,128)(2,1)S(1)}, bf16[130,16,128]{2,1,0:T(8,128)(2,1)S(1)}, u32[]{:S(2)}, u32[]{:S(2)}) collective-permute-start(bf16[130,16,128]{2,1,0:T(8,128)(2,1)S(1)} %pad_maximum_fusion.1), channel_id=1, source_target_pairs={{0,10},{8,0},{1,43},{9,33},{16,11},{24,1},{17,42},{25,32},{32,31},... | collective-permute-start | bytes 1597448 | tf_op jit(solution)/shard_map/ppermute | solution.py:188
  20.4 1.4 collective-permute-start.4
  21.8 0.8 collective-permute-start.5
  22.6 0.1 pad_maximum_fusion.4
  22.7 7.2 %collective-permute-start.6 = (bf16[130,3,128]{2,1,0:T(4,128)(2,1)S(1)}, bf16[130,3,128]{2,1,0:T(4,128)(2,1)S(1)}, u32[]{:S(2)}, u32[]{:S(2)}) collective-permute-start(bf16[130,3,128]{2,1,0:T(4,128)(2,1)S(1)} %pad_maximum_fusion.4), channel_id=1, source_target_pairs={{16,0},{17,33},{48,1},{49,32},{80,6},{81,39},{112,7},{113,38},{144... | collective-permute-start | bytes 299528 | tf_op jit(solution)/shard_map/ppermute | solution.py:198
  29.9 0.1 pad_maximum_fusion.5
  30.0 10.1 %collective-permute-done.6.refs_4_ = bf16[130,3,128]{2,1,0:T(4,128)(2,1)S(1)} collective-permute-done((bf16[130,3,128]{2,1,0:T(4,128)(2,1)S(1)}, bf16[130,3,128]{2,1,0:T(4,128)(2,1)S(1)}, u32[]{:S(2)}, u32[]{:S(2)}) %collective-permute-start.6) | collective-permute-done | bytes 99872 | tf_op jit(solution)/shard_map/ppermute | solution.py:198
  40.1 1.3 collective-permute-start.7
  41.3 0.1 pad_maximum_fusion.6
  41.4 2.4 %collective-permute-done.7.refs_5_ = bf16[130,3,128]{2,1,0:T(4,128)(2,1)S(1)} collective-permute-done((bf16[130,3,128]{2,1,0:T(4,128)(2,1)S(1)}, bf16[130,3,128]{2,1,0:T(4,128)(2,1)S(1)}, u32[]{:S(2)}, u32[]{:S(2)}) %collective-permute-start.7) | collective-permute-done | bytes 99872 | tf_op jit(solution)/shard_map/ppermute | solution.py:198
  43.9 1.9 %collective-permute-start.8 = (bf16[130,3,128]{2,1,0:T(4,128)(2,1)S(1)}, bf16[130,3,128]{2,1,0:T(4,128)(2,1)S(1)}, u32[]{:S(2)}, u32[]{:S(2)}) collective-permute-start(bf16[130,3,128]{2,1,0:T(4,128)(2,1)S(1)} %pad_maximum_fusion.6), channel_id=1, source_target_pairs={{16,20},{17,53},{48,21},{49,52},{80,18},{81,51},{112,19},{113,50},... | collective-permute-start | bytes 299528 | tf_op jit(solution)/shard_map/ppermute | solution.py:198
  45.8 0.1 pad_maximum_fusion.7
  45.9 20.0 %collective-permute-done.8.refs_6_ = bf16[130,3,128]{2,1,0:T(4,128)(2,1)S(1)} collective-permute-done((bf16[130,3,128]{2,1,0:T(4,128)(2,1)S(1)}, bf16[130,3,128]{2,1,0:T(4,128)(2,1)S(1)}, u32[]{:S(2)}, u32[]{:S(2)}) %collective-permute-start.8) | collective-permute-done | bytes 99872 | tf_op jit(solution)/shard_map/ppermute | solution.py:198
  65.9 1.3 collective-permute-start.9
  67.2 0.6 pad_add_fusion.1.where_ref
  67.8 1.9 %collective-permute-done.9.refs_7_ = bf16[130,3,128]{2,1,0:T(4,128)(2,1)S(1)} collective-permute-done((bf16[130,3,128]{2,1,0:T(4,128)(2,1)S(1)}, bf16[130,3,128]{2,1,0:T(4,128)(2,1)S(1)}, u32[]{:S(2)}, u32[]{:S(2)}) %collective-permute-start.9) | collective-permute-done | bytes 99872 | tf_op jit(solution)/shard_map/ppermute | solution.py:198
  69.7 0.0 collective-permute-done.2.refs_0_
  69.7 0.0 collective-permute-done.3.refs_1_
  69.7 0.0 copy-start.5
  69.7 0.0 collective-permute-done.4.refs_2_
  69.7 0.0 collective-permute-done.5.refs_3_
  69.7 0.8 copy-done.4
  70.5 0.2 copy-done.6
  70.7 0.0 copy-done.11
  70.7 0.2 copy-done.5
  70.9 0.6 copy-done.7
  71.5 7.6 %filterbank.1 = bf16[8,65,32,128]{3,2,1,0:T(8,128)(2,1)} custom-call(s32[3]{0:T(128)} %pad_add_fusion.1.where_ref, bf16[130,16,128]{2,1,0:T(8,128)(2,1)} %copy-done.4, bf16[130,16,128]{2,1,0:T(8,128)(2,1)} %copy-done.5, bf16[130,16,128]{2,1,0:T(8,128)(2,1)} %copy-done.6, bf16[130,16,128]{2,1,0:T(8,128)(2,1)} %copy-done.7, bf16[130,3,128]{2,1,0:T(4,128)(2,1)} %copy-done.8, ...), custom_call_target="tpu_custom_call" | custom-call | flops 2181038080 | bytes 6291456 | tf_op jit(solution)/shard_map/filterbank/pallas_call | solution.py:230
  79.1 39.6 %all-to-all-start = ((bf16[8,65,32,128]{3,2,1,0:T(8,128)(2,1)}), bf16[8,65,32,128]{3,2,1,0:T(8,128)(2,1)}, u32[]{:S(2)}, u32[]{:S(2)}) async-start(bf16[8,65,32,128]{3,2,1,0:T(8,128)(2,1)} %filterbank.1), calls=%async_computation | async-start | bytes 8519680 | tf_op jit(solution)/shard_map/all_to_all | solution.py:241
  118.7 0.1 concatenate.67
  118.8 0.1 dynamic_slice.39
  118.8 0.1 slice.73
  118.9 0.1 copy.31
  119.0 0.8 reshape.64.kern_ref
  119.8 0.0 copy-done
  119.8 0.2 select_reduce_fusion
  120.0 0.1 fusion
  120.1 0.6 pad_add_fusion.flag_ref
  120.7 9.5 %weights.1.w_ref = bf16[16,256,960]{2,1,0:T(8,128)(2,1)} custom-call(s32[3,128]{1,0:T(4,128)} %pad_add_fusion.flag_ref, bf16[64,288]{1,0:T(8,128)(2,1)} %reshape.64.kern_ref), custom_call_target="tpu_custom_call" | custom-call | flops 283115520 | bytes 8388608 | tf_op jit(solution)/shard_map/weights/pallas_call | solution.py:212
  130.2 0.6 xor_add_fusion.slot_ref
  130.7 38.3 %all-to-all-done.recv_ref = bf16[8,65,32,128]{3,2,1,0:T(8,128)(2,1)} async-done(((bf16[8,65,32,128]{3,2,1,0:T(8,128)(2,1)}), bf16[8,65,32,128]{3,2,1,0:T(8,128)(2,1)}, u32[]{:S(2)}, u32[]{:S(2)}) %all-to-all-start) | async-done | bytes 4259872 | tf_op jit(solution)/shard_map/all_to_all | solution.py:241
  169.0 17.6 %conv.1 = bf16[128,32,512]{2,1,0:T(8,128)(2,1)} custom-call(s32[8]{0:T(128)} %xor_add_fusion.slot_ref, bf16[8,65,32,128]{3,2,1,0:T(8,128)(2,1)} %all-to-all-done.recv_ref, bf16[16,256,960]{2,1,0:T(8,128)(2,1)} %weights.1.w_ref), custom_call_target="tpu_custom_call" | custom-call | flops 4026531840 | bytes 16777216 | tf_op jit(solution)/shard_map/conv/pallas_call | solution.py:245
  (32 shorter events, 0.3 us)
Async XLA Ops:
  0.0 119.8 %copy-start = (s32[128,8]{0,1:T(8,128)S(1)}, s32[128,8]{0,1:T(8,128)}, u32[]{:S(2)}) copy-start(s32[128,8]{0,1:T(8,128)} %param.9) | copy-start | bytes 12292
  0.0 9.7 %copy-start.1 = (bf16[512,256]{1,0:T(8,128)(2,1)S(1)}, bf16[512,256]{1,0:T(8,128)(2,1)}, u32[]{:S(2)}) copy-start(bf16[512,256]{1,0:T(8,128)(2,1)} %param.7) | copy-start | bytes 786436
  1.0 11.2 %collective-permute-start.1 = (bf16[1,2048]{1,0:T(2,128)(2,1)S(1)}, bf16[1,2048]{1,0:T(2,128)(2,1)S(1)}, u32[]{:S(2)}, u32[]{:S(2)}) collective-permute-start(bf16[1,2048]{1,0:T(2,128)(2,1)S(1)} %get-tuple-element.13), channel_id=1, source_target_pairs={{1,0},{2,1},{3,2},{4,3},{5,4},{6,5},{7,6},{9,8},{10,9},{11,10},{12... | collective-permute-start | bytes 12296 | tf_op jit(solution)/shard_map/ppermute | solution.py:171
  4.8 7.4 %collective-permute-start = (bf16[1,2048]{1,0:T(2,128)(2,1)S(1)}, bf16[1,2048]{1,0:T(2,128)(2,1)S(1)}, u32[]{:S(2)}, u32[]{:S(2)}) collective-permute-start(bf16[1,2048]{1,0:T(2,128)(2,1)S(1)} %get-tuple-element.20), channel_id=1, source_target_pairs={{0,1},{1,2},{2,3},{3,4},{4,5},{5,6},{6,7},{8,9},{9,10},{10,11},{11... | collective-permute-start | bytes 12296 | tf_op jit(solution)/shard_map/ppermute | solution.py:170
  12.6 57.1 %collective-permute-start.2 = (bf16[130,16,128]{2,1,0:T(8,128)(2,1)S(1)}, bf16[130,16,128]{2,1,0:T(8,128)(2,1)S(1)}, u32[]{:S(2)}, u32[]{:S(2)}) collective-permute-start(bf16[130,16,128]{2,1,0:T(8,128)(2,1)S(1)} %pad_maximum_fusion), channel_id=1, source_target_pairs={{0,0},{8,10},{1,33},{9,43},{16,1},{24,11},{17,32},{25,42},{32,21},... | collective-permute-start | bytes 1597448 | tf_op jit(solution)/shard_map/ppermute | solution.py:188
  14.6 55.1 %collective-permute-start.3 = (bf16[130,16,128]{2,1,0:T(8,128)(2,1)S(1)}, bf16[130,16,128]{2,1,0:T(8,128)(2,1)S(1)}, u32[]{:S(2)}, u32[]{:S(2)}) collective-permute-start(bf16[130,16,128]{2,1,0:T(8,128)(2,1)S(1)} %pad_maximum_fusion.1), channel_id=1, source_target_pairs={{0,10},{8,0},{1,43},{9,33},{16,11},{24,1},{17,42},{25,32},{32,31},... | collective-permute-start | bytes 1597448 | tf_op jit(solution)/shard_map/ppermute | solution.py:188
  20.4 49.3 %collective-permute-start.4 = (bf16[130,16,128]{2,1,0:T(8,128)(2,1)S(1)}, bf16[130,16,128]{2,1,0:T(8,128)(2,1)S(1)}, u32[]{:S(2)}, u32[]{:S(2)}) collective-permute-start(bf16[130,16,128]{2,1,0:T(8,128)(2,1)S(1)} %pad_maximum_fusion.2), channel_id=1, source_target_pairs={{0,20},{8,30},{1,53},{9,63},{16,21},{24,31},{17,52},{25,62},{32,1}... | collective-permute-start | bytes 1597448 | tf_op jit(solution)/shard_map/ppermute | solution.py:188
  21.8 47.9 %collective-permute-start.5 = (bf16[130,16,128]{2,1,0:T(8,128)(2,1)S(1)}, bf16[130,16,128]{2,1,0:T(8,128)(2,1)S(1)}, u32[]{:S(2)}, u32[]{:S(2)}) collective-permute-start(bf16[130,16,128]{2,1,0:T(8,128)(2,1)S(1)} %pad_maximum_fusion.3), channel_id=1, source_target_pairs={{0,30},{8,20},{1,63},{9,53},{16,31},{24,21},{17,62},{25,52},{32,11... | collective-permute-start | bytes 1597448 | tf_op jit(solution)/shard_map/ppermute | solution.py:188
  22.7 17.3 %collective-permute-start.6 = (bf16[130,3,128]{2,1,0:T(4,128)(2,1)S(1)}, bf16[130,3,128]{2,1,0:T(4,128)(2,1)S(1)}, u32[]{:S(2)}, u32[]{:S(2)}) collective-permute-start(bf16[130,3,128]{2,1,0:T(4,128)(2,1)S(1)} %pad_maximum_fusion.4), channel_id=1, source_target_pairs={{16,0},{17,33},{48,1},{49,32},{80,6},{81,39},{112,7},{113,38},{144... | collective-permute-start | bytes 299528 | tf_op jit(solution)/shard_map/ppermute | solution.py:198
  40.1 30.7 %copy-start.8 = (bf16[130,3,128]{2,1,0:T(4,128)(2,1)}, bf16[130,3,128]{2,1,0:T(4,128)(2,1)S(1)}, u32[]{:S(2)}) copy-start(bf16[130,3,128]{2,1,0:T(4,128)(2,1)S(1)} %collective-permute-done.6.refs_4_) | copy-start | bytes 299524
  40.1 3.8 %collective-permute-start.7 = (bf16[130,3,128]{2,1,0:T(4,128)(2,1)S(1)}, bf16[130,3,128]{2,1,0:T(4,128)(2,1)S(1)}, u32[]{:S(2)}, u32[]{:S(2)}) collective-permute-start(bf16[130,3,128]{2,1,0:T(4,128)(2,1)S(1)} %pad_maximum_fusion.5), channel_id=1, source_target_pairs={{16,10},{17,43},{48,11},{49,42},{80,8},{81,41},{112,9},{113,40},{1... | collective-permute-start | bytes 299528 | tf_op jit(solution)/shard_map/ppermute | solution.py:198
  43.9 26.8 %copy-start.9 = (bf16[130,3,128]{2,1,0:T(4,128)(2,1)}, bf16[130,3,128]{2,1,0:T(4,128)(2,1)S(1)}, u32[]{:S(2)}) copy-start(bf16[130,3,128]{2,1,0:T(4,128)(2,1)S(1)} %collective-permute-done.7.refs_5_) | copy-start | bytes 299524
  43.9 22.0 %collective-permute-start.8 = (bf16[130,3,128]{2,1,0:T(4,128)(2,1)S(1)}, bf16[130,3,128]{2,1,0:T(4,128)(2,1)S(1)}, u32[]{:S(2)}, u32[]{:S(2)}) collective-permute-start(bf16[130,3,128]{2,1,0:T(4,128)(2,1)S(1)} %pad_maximum_fusion.6), channel_id=1, source_target_pairs={{16,20},{17,53},{48,21},{49,52},{80,18},{81,51},{112,19},{113,50},... | collective-permute-start | bytes 299528 | tf_op jit(solution)/shard_map/ppermute | solution.py:198
  65.9 4.8 %copy-start.10 = (bf16[130,3,128]{2,1,0:T(4,128)(2,1)}, bf16[130,3,128]{2,1,0:T(4,128)(2,1)S(1)}, u32[]{:S(2)}) copy-start(bf16[130,3,128]{2,1,0:T(4,128)(2,1)S(1)} %collective-permute-done.8.refs_6_) | copy-start | bytes 299524
  65.9 3.8 %collective-permute-start.9 = (bf16[130,3,128]{2,1,0:T(4,128)(2,1)S(1)}, bf16[130,3,128]{2,1,0:T(4,128)(2,1)S(1)}, u32[]{:S(2)}, u32[]{:S(2)}) collective-permute-start(bf16[130,3,128]{2,1,0:T(4,128)(2,1)S(1)} %pad_maximum_fusion.7), channel_id=1, source_target_pairs={{16,30},{17,63},{48,31},{49,62},{80,28},{81,61},{112,29},{113,60},... | collective-permute-start | bytes 299528 | tf_op jit(solution)/shard_map/ppermute | solution.py:198
  69.7 1.0 copy-start.11
  69.7 0.8 copy-start.4
  69.7 1.2 copy-start.5
  69.7 1.0 copy-start.6
  70.7 0.8 copy-start.7
  79.1 39.6 %copy-start.3 = (s32[4096]{0:T(1024)S(1)}, s32[4096]{0:T(1024)}, u32[]{:S(2)}) copy-start(s32[4096]{0:T(1024)} %param.8) | copy-start | bytes 49156
  79.1 39.8 %copy-start.2 = (bf16[2,1,3,3,32,32]{5,4,3,2,1,0:T(8,128)(2,1)S(1)}, bf16[2,1,3,3,32,32]{5,4,3,2,1,0:T(8,128)(2,1)}, u32[]{:S(2)}) copy-start(bf16[2,1,3,3,32,32]{5,4,3,2,1,0:T(8,128)(2,1)} %param.10) | copy-start | bytes 110596
  79.1 89.9 %all-to-all-start = ((bf16[8,65,32,128]{3,2,1,0:T(8,128)(2,1)}), bf16[8,65,32,128]{3,2,1,0:T(8,128)(2,1)}, u32[]{:S(2)}, u32[]{:S(2)}) async-start(bf16[8,65,32,128]{3,2,1,0:T(8,128)(2,1)} %filterbank.1), calls=%async_computation | async-start | bytes 8519680 | tf_op jit(solution)/shard_map/all_to_all | solution.py:241

commit v2 on v1

--- a/solution.py
+++ b/solution.py
@@ -41,31 +41,35 @@
 
 
 def filter_kernel(where_ref, *refs):
-    pieces, rims, (taps_ref, out_ref, seq_ref) = refs[:4], refs[4:8], refs[8:]
+    pieces, edges, rims, (taps_ref, out_ref, seq_ref) = refs[:4], refs[4:8], refs[8:12], refs[12:]
     first, core, keep = where_ref[0], where_ref[1], where_ref[2]
-    chans = seq_ref.shape[0]
-
-    @pl.loop(0, pieces[0].shape[0] // chans)
-    def _(i):
-        rows = pl.ds(i * chans, chans)
-        for j, ref in enumerate(pieces):
+
+    def filtered(parts, rows, chans, place):
+        for j, ref in enumerate(parts):
             at = (first ^ (j >> 1)) * 48 + (core ^ (j & 1)) * 16
-            seq_ref[:, pl.ds(pl.multiple_of(at, 16), 16), :] = ref[rows]
-        seq_ref[:, 32:48, :] = seq_ref[:, 48:64, :] * keep.astype(jnp.bfloat16)
-        seq_ref[:, 80:83, :] = (rims[0][rows] + rims[1][rows]) + (rims[2][rows] + rims[3][rows])
+            seq_ref[:chans, pl.ds(pl.multiple_of(at, 16), 16), :] = ref[rows]
+        seq_ref[:chans, 32:48, :] = seq_ref[:chans, 48:64, :] * keep.astype(jnp.bfloat16)
+        rim = (rims[0][place] + rims[1][place]) + (rims[2][place] + rims[3][place])
+        seq_ref[:chans, 80:83, :] = rim
         columns = []
         for k in range(4):
-            runs = [seq_ref[:, s + k : s + k + 32, :] for s in (0, 48)]
+            runs = [seq_ref[:chans, s + k : s + k + 32, :] for s in (0, 48)]
             columns.append(jnp.concatenate(runs, axis=1).reshape(chans * 64, HOP))
         frames = jnp.concatenate(columns, axis=1)
-        feats = lax.dot_general(
+        return lax.dot_general(
             taps_ref[...], frames, (((1,), (1,)), ((), ())), preferred_element_type=jnp.float32
         ).astype(jnp.bfloat16)
+
+    @pl.loop(0, 8)
+    def _(i):
+        feats = filtered(pieces, pl.ds(i * 16, 16), 16, pl.ds(i * 16, 16))
         for g in range(8):
-            for p in range(chans // 2):
-                out_ref[g, i * (chans // 2) + p] = feats[
-                    g * GW : (g + 1) * GW, p * 128 : (p + 1) * 128
-                ]
+            for p in range(8):
+                out_ref[g, i * 8 + p] = feats[g * GW : (g + 1) * GW, p * 128 : (p + 1) * 128]
+
+    feats = filtered(edges, slice(0, 2), 2, slice(128, 130))
+    for g in range(8):
+        out_ref[g, 64] = feats[g * GW : (g + 1) * GW, :]
 
 
 def weight_kernel(flag_ref, kern_ref, out_ref, base_ref):
@@ -166,36 +170,39 @@
     turn = 2 * z1 + core
     vmem = pl.BlockSpec(memory_space=pltpu.VMEM)
 
+    def send(part, perm, axes=AXES):
+        return lax.ppermute(part, axes, perm)
+
+    steps = [(s, w) for s in (0, 1) for w in (0, 1)]
+    place = {(s, w): 2 * (s ^ z2) + (core ^ w) for s, w in steps}
+
+    def bulk(wave, s, w):
+        part = lax.dynamic_slice_in_dim(wave, 128 * place[s, w], 128, 0).reshape(128, 16, HOP)
+        return send(part, bulk_route(s, w))
+
+    pieces = [bulk(waveform, 0, 0), bulk(waveform, 0, 1)]
     up = [(i, i + 1) for i in range(7)]
-    row_low = lax.ppermute(waveform[511:], "fiber", up)
-    row_high = lax.ppermute(waveform[:1], "fiber", [(j, i) for i, j in up])
-    edge_rows = jnp.concatenate(
-        [row_low]
-        + [waveform[i : i + 1] for i in (128, 127, 256, 255, 384, 383)]
-        + [row_high],
-        axis=0,
+    row_low = send(waveform[511:], up, "fiber")
+    row_high = send(waveform[:1], [(j, i) for i, j in up], "fiber")
+    wave, row_low, row_high = lax.optimization_barrier((waveform, row_low, row_high))
+    rows = jnp.concatenate(
+        [row_low] + [wave[i : i + 1] for i in (128, 127, 256, 255, 384, 383)] + [row_high], axis=0
     ).reshape(4, 2, 2048)
-
-    def block_rows(at):
-        main = lax.dynamic_slice_in_dim(waveform, 128 * at, 128, 0)
-        sides = lax.dynamic_index_in_dim(edge_rows, at, 0, False)
-        return main.reshape(128, 16, HOP), sides.reshape(2, 16, HOP)
-
-    pieces, rims = [], []
-    for step in (0, 1):
-        for swap in (0, 1):
-            part = jnp.concatenate(block_rows(2 * (step ^ z2) + (core ^ swap)), axis=0)
-            pieces.append(lax.ppermute(part, AXES, bulk_route(step, swap)))
-    for b in (0, 1):
-        for c in (0, 1):
-            part = jnp.concatenate(
-                [
-                    waveform[128 * (2 * b + c) : 128 * (2 * b + c + 1), : 3 * HOP],
-                    edge_rows[2 * b + c, :, : 3 * HOP],
-                ],
-                axis=0,
-            ).reshape(130, 3, HOP)
-            rims.append(lax.ppermute(part, AXES, rim_route(b, c)))
+    rims = []
+    for b, c in steps:
+        at = 2 * b + c
+        part = jnp.concatenate(
+            [wave[128 * at : 128 * (at + 1), : 3 * HOP], rows[at, :, : 3 * HOP]], axis=0
+        ).reshape(130, 3, HOP)
+        rims.append(send(part, rim_route(b, c)))
+    pieces += [bulk(wave, 1, 0), bulk(wave, 1, 1)]
+    edges = [
+        send(
+            lax.dynamic_index_in_dim(rows, place[s, w], 0, False).reshape(2, 16, HOP),
+            bulk_route(s, w),
+        )
+        for s, w in steps
+    ]
 
     edge = jnp.array([-1], jnp.int32)
     sec = lax.dynamic_slice_in_dim(
@@ -230,14 +237,14 @@
     feats = pl.pallas_call(
         filter_kernel,
         out_shape=jax.ShapeDtypeStruct((8, 65, GW, 128), jnp.bfloat16),
-        in_specs=[pl.BlockSpec(memory_space=pltpu.SMEM)] + [vmem] * 9,
+        in_specs=[pl.BlockSpec(memory_space=pltpu.SMEM)] + [vmem] * 13,
         out_specs=vmem,
-        scratch_shapes=[pltpu.VMEM((26, 96, HOP), jnp.bfloat16)],
+        scratch_shapes=[pltpu.VMEM((16, 96, HOP), jnp.bfloat16)],
         cost_estimate=pl.CostEstimate(
             flops=2 * 8320 * 512 * 256, bytes_accessed=6 << 20, transcendentals=0
         ),
         name="filterbank",
-    )(where, *pieces, *rims, filters.T)
+    )(where, *pieces, *edges, *rims, filters.T)
     recv = lax.all_to_all(feats, "fiber", 0, 0, tiled=True)
 
     q = jnp.arange(8, dtype=jnp.int32)

time: 187 us -> 174 us (0.930)
  the two profiles are of different devices: /device:TPU:92 before, /device:TPU:72 now
where the time goes in v2:
time: 174 us; the launch traced here: 173 us
  waiting for transfers between devices  70.9 us (41%)
  starting transfers between devices  50 us (29%)
  Pallas kernels  35.3 us (20%)
  local copies, waits for them, and re-layouts  14.1 us (8%)
  other arithmetic  2.32 us (1%)
    ppermute x14, starting transfers between devices, send(): return lax.ppermute(part, axes, perm)  42 us
    all_to_all x1, waiting for transfers between devices, shards(): recv = lax.all_to_all(feats, 'fiber', 0, 0, tiled=True)  35.7 us
    ppermute x14, waiting for transfers between devices, send(): return lax.ppermute(part, axes, perm)  35.1 us
    pallas_call x1, Pallas kernels, shards(): pl.pallas_call(conv_kernel, out_shape=jax.ShapeDtypeStruct((128, GW, 512)...  17.6 us
    pallas_call x1, Pallas kernels, shards(): pl.pallas_call(weight_kernel, out_shape=jax.ShapeDtypeStruct((16, 256, 96...  9.45 us
    pallas_call x1, Pallas kernels, shards(): pl.pallas_call(filter_kernel, out_shape=jax.ShapeDtypeStruct((8, 65, GW,...  8.28 us
    all_to_all x1, starting transfers between devices, shards(): recv = lax.all_to_all(feats, 'fiber', 0, 0, tiled=True)  7.98 us
    unnamed x40, local copies, waits for them, and re-layouts  6.58 us
  transfers between devices with their start and end apart: 15, of which 6 were waited for; matrix products, arithmetic and copies ran while one was open for 8% of the time, Pallas kernels for 5%

profile of v2, /device:TPU:72, one launch (start us, length us, event | category | flops | bytes accessed | tf_op | source)
XLA Modules:
  0.0 173.0 jit_solution(1819680400243332709)
XLA Ops:
  0.0 0.8 fusion.5
  0.8 1.3 collective-permute-start.3
  2.1 4.5 %collective-permute-start.2 = (bf16[1,2048]{1,0:T(2,128)(2,1)S(1)}, bf16[1,2048]{1,0:T(2,128)(2,1)S(1)}, u32[]{:S(2)}, u32[]{:S(2)}) collective-permute-start(bf16[1,2048]{1,0:T(2,128)(2,1)S(1)} %get-tuple-element.24), channel_id=1, source_target_pairs={{0,1},{1,2},{2,3},{3,4},{4,5},{5,6},{6,7},{8,9},{9,10},{10,11},{11... | collective-permute-start | bytes 12296 | tf_op jit(solution)/shard_map/ppermute | solution.py:174
  6.7 0.0 copy-start.2
  6.7 0.0 copy-start.1
  6.7 1.4 dynamic-slice_bitcast_fusion.2
  8.1 0.9 copy.33
  9.0 1.9 %collective-permute-start = (bf16[128,16,128]{2,1,0:T(8,128)(2,1)}, bf16[128,16,128]{2,1,0:T(8,128)(2,1)}, u32[]{:S(2)}, u32[]{:S(2)}) collective-permute-start(bf16[128,16,128]{2,1,0:T(8,128)(2,1)} %bitcast.16), channel_id=1, source_target_pairs={{0,0},{8,10},{1,33},{9,43},{16,1},{24,11},{17,32},{25,42},{32,21},... | collective-permute-start | bytes 1572872 | tf_op jit(solution)/shard_map/ppermute | solution.py:174
  10.9 0.9 copy.34
  11.9 6.7 %collective-permute-start.1 = (bf16[128,16,128]{2,1,0:T(8,128)(2,1)}, bf16[128,16,128]{2,1,0:T(8,128)(2,1)}, u32[]{:S(2)}, u32[]{:S(2)}) collective-permute-start(bf16[128,16,128]{2,1,0:T(8,128)(2,1)} %bitcast.18), channel_id=1, source_target_pairs={{0,10},{8,0},{1,43},{9,33},{16,11},{24,1},{17,42},{25,32},{32,31},... | collective-permute-start | bytes 1572872 | tf_op jit(solution)/shard_map/ppermute | solution.py:174
  18.6 0.8 copy.28
  19.4 0.0 collective-permute-done.3
  19.4 0.0 collective-permute-done.2
  19.5 2.5 %copy.20 = bf16[512,2048]{0,1:T(8,128)(2,1)} copy(bf16[512,2048]{1,0:T(8,128)(2,1)S(1)} %copy-done.1) | data formatting | bytes 4194304 | tf_op jit(solution)/shard_map/optimization_barrier | solution.py:187
  22.0 0.1 concatenate.38
  22.1 0.6 fusion.6
  22.7 0.6 copy.47
  23.3 0.6 copy.48
  23.9 5.8 %collective-permute-start.6 = (bf16[2,16,128]{2,1,0:T(8,128)(2,1)}, bf16[2,16,128]{2,1,0:T(8,128)(2,1)}, u32[]{:S(2)}, u32[]{:S(2)}) collective-permute-start(bf16[2,16,128]{2,1,0:T(8,128)(2,1)} %bitcast.53), channel_id=1, source_target_pairs={{0,0},{8,10},{1,33},{9,43},{16,1},{24,11},{17,32},{25,42},{32,21},... | collective-permute-start | bytes 24584 | tf_op jit(solution)/shard_map/ppermute | solution.py:174
  29.8 2.1 %collective-permute-start.7 = (bf16[2,16,128]{2,1,0:T(8,128)(2,1)}, bf16[2,16,128]{2,1,0:T(8,128)(2,1)}, u32[]{:S(2)}, u32[]{:S(2)}) collective-permute-start(bf16[2,16,128]{2,1,0:T(8,128)(2,1)} %bitcast.52), channel_id=1, source_target_pairs={{0,10},{8,0},{1,43},{9,33},{16,11},{24,1},{17,42},{25,32},{32,31},... | collective-permute-start | bytes 24584 | tf_op jit(solution)/shard_map/ppermute | solution.py:174
  31.9 4.6 %collective-permute-start.8 = (bf16[2,16,128]{2,1,0:T(8,128)(2,1)S(1)}, bf16[2,16,128]{2,1,0:T(8,128)(2,1)}, u32[]{:S(2)}, u32[]{:S(2)}) collective-permute-start(bf16[2,16,128]{2,1,0:T(8,128)(2,1)S(1)} %bitcast.62), channel_id=1, source_target_pairs={{0,20},{8,30},{1,53},{9,63},{16,21},{24,31},{17,52},{25,62},{32,1}... | collective-permute-start | bytes 24584 | tf_op jit(solution)/shard_map/ppermute | solution.py:174
  36.4 1.1 fusion.3
  37.5 0.1 dynamic-slice_bitcast_fusion
  37.7 0.7 concatenate.40
  38.3 0.1 copy.36
  38.5 0.1 copy.35
  38.6 0.1 copy.21
  38.7 4.7 %collective-permute-done.6.refs_4_ = bf16[2,16,128]{2,1,0:T(8,128)(2,1)} collective-permute-done((bf16[2,16,128]{2,1,0:T(8,128)(2,1)}, bf16[2,16,128]{2,1,0:T(8,128)(2,1)}, u32[]{:S(2)}, u32[]{:S(2)}) %collective-permute-start.6) | collective-permute-done | bytes 8224 | tf_op jit(solution)/shard_map/ppermute | solution.py:174
  43.5 2.9 %collective-permute-start.9 = (bf16[2,16,128]{2,1,0:T(8,128)(2,1)S(1)}, bf16[2,16,128]{2,1,0:T(8,128)(2,1)S(1)}, u32[]{:S(2)}, u32[]{:S(2)}) collective-permute-start(bf16[2,16,128]{2,1,0:T(8,128)(2,1)S(1)} %bitcast.63), channel_id=1, source_target_pairs={{0,30},{8,20},{1,63},{9,53},{16,31},{24,21},{17,62},{25,52},{32,11... | collective-permute-start | bytes 24584 | tf_op jit(solution)/shard_map/ppermute | solution.py:174
  46.4 6.4 %collective-permute-start.5 = (bf16[128,16,128]{2,1,0:T(8,128)(2,1)S(1)}, bf16[128,16,128]{2,1,0:T(8,128)(2,1)S(1)}, u32[]{:S(2)}, u32[]{:S(2)}) collective-permute-start(bf16[128,16,128]{2,1,0:T(8,128)(2,1)S(1)} %bitcast.54), channel_id=1, source_target_pairs={{0,30},{8,20},{1,63},{9,53},{16,31},{24,21},{17,62},{25,52},{32,11... | collective-permute-start | bytes 1572872 | tf_op jit(solution)/shard_map/ppermute | solution.py:174
  52.8 0.1 pad_maximum_fusion
  52.9 0.1 copy.25
  53.1 0.1 copy.27
  53.2 0.1 copy.23
  53.4 1.3 collective-permute-start.10
  54.7 0.1 pad_maximum_fusion.1
  54.8 17.6 %collective-permute-done.10.refs_8_ = bf16[130,3,128]{2,1,0:T(4,128)(2,1)S(1)} collective-permute-done((bf16[130,3,128]{2,1,0:T(4,128)(2,1)S(1)}, bf16[130,3,128]{2,1,0:T(4,128)(2,1)S(1)}, u32[]{:S(2)}, u32[]{:S(2)}) %collective-permute-start.10) | collective-permute-done | bytes 99872 | tf_op jit(solution)/shard_map/ppermute | solution.py:174
  72.4 1.3 collective-permute-start.11
  73.7 0.1 pad_maximum_fusion.3
  73.8 2.6 %collective-permute-done.11.refs_9_ = bf16[130,3,128]{2,1,0:T(4,128)(2,1)S(1)} collective-permute-done((bf16[130,3,128]{2,1,0:T(4,128)(2,1)S(1)}, bf16[130,3,128]{2,1,0:T(4,128)(2,1)S(1)}, u32[]{:S(2)}, u32[]{:S(2)}) %collective-permute-start.11) | collective-permute-done | bytes 99872 | tf_op jit(solution)/shard_map/ppermute | solution.py:174
  76.3 1.3 collective-permute-start.13
  77.6 0.1 pad_maximum_fusion.2
  77.7 2.4 %collective-permute-done.13.refs_11_ = bf16[130,3,128]{2,1,0:T(4,128)(2,1)S(1)} collective-permute-done((bf16[130,3,128]{2,1,0:T(4,128)(2,1)S(1)}, bf16[130,3,128]{2,1,0:T(4,128)(2,1)S(1)}, u32[]{:S(2)}, u32[]{:S(2)}) %collective-permute-start.13) | collective-permute-done | bytes 99872 | tf_op jit(solution)/shard_map/ppermute | solution.py:174
  80.1 1.9 %collective-permute-start.12 = (bf16[130,3,128]{2,1,0:T(4,128)(2,1)S(1)}, bf16[130,3,128]{2,1,0:T(4,128)(2,1)S(1)}, u32[]{:S(2)}, u32[]{:S(2)}) collective-permute-start(bf16[130,3,128]{2,1,0:T(4,128)(2,1)S(1)} %pad_maximum_fusion.2), channel_id=1, source_target_pairs={{16,20},{17,53},{48,21},{49,52},{80,18},{81,51},{112,19},{113,50},... | collective-permute-start | bytes 299528 | tf_op jit(solution)/shard_map/ppermute | solution.py:174
  82.1 0.6 pad_add_fusion.1.where_ref
  82.7 7.8 %collective-permute-done.12.refs_10_ = bf16[130,3,128]{2,1,0:T(4,128)(2,1)S(1)} collective-permute-done((bf16[130,3,128]{2,1,0:T(4,128)(2,1)S(1)}, bf16[130,3,128]{2,1,0:T(4,128)(2,1)S(1)}, u32[]{:S(2)}, u32[]{:S(2)}) %collective-permute-start.12) | collective-permute-done | bytes 99872 | tf_op jit(solution)/shard_map/ppermute | solution.py:174
  90.5 0.0 copy-start.7
  90.6 0.6 copy-done.12
  91.1 0.2 copy-done.7
  91.3 0.2 copy-done.8
  91.5 8.3 %filterbank.1 = bf16[8,65,32,128]{3,2,1,0:T(8,128)(2,1)} custom-call(s32[3]{0:T(128)} %pad_add_fusion.1.where_ref, bf16[128,16,128]{2,1,0:T(8,128)(2,1)} %collective-permute-done.refs_0_, bf16[128,16,128]{2,1,0:T(8,128)(2,1)} %collective-permute-done.1.refs_1_, bf16[128,16,128]{2,1,0:T(8,128)(2,1)} %copy-done.7, bf16[128,16,128]{2,1,0:T(8,128)(2,1)} %copy-done.8, ...), custom_call_target="tpu_custom_call" | custom-call | flops 2181038080 | bytes 6291456 | tf_op jit(solution)/shard_map/filterbank/pallas_call | solution.py:237
  99.8 8.0 %all-to-all-start = ((bf16[8,65,32,128]{3,2,1,0:T(8,128)(2,1)}), bf16[8,65,32,128]{3,2,1,0:T(8,128)(2,1)}, u32[]{:S(2)}, u32[]{:S(2)}) async-start(bf16[8,65,32,128]{3,2,1,0:T(8,128)(2,1)} %filterbank.1), calls=%async_computation | async-start | bytes 8519680 | tf_op jit(solution)/shard_map/all_to_all | solution.py:248
  107.8 0.1 concatenate.51
  107.8 0.1 dynamic_slice.39
  107.9 0.1 slice.73
  108.0 0.1 copy.31
  108.1 0.8 reshape.64.kern_ref
  108.9 0.2 select_reduce_fusion
  109.1 0.1 fusion
  109.1 0.6 pad_add_fusion.flag_ref
  109.7 9.5 %weights.1.w_ref = bf16[16,256,960]{2,1,0:T(8,128)(2,1)} custom-call(s32[3,128]{1,0:T(4,128)} %pad_add_fusion.flag_ref, bf16[64,288]{1,0:T(8,128)(2,1)} %reshape.64.kern_ref), custom_call_target="tpu_custom_call" | custom-call | flops 283115520 | bytes 8388608 | tf_op jit(solution)/shard_map/weights/pallas_call | solution.py:219
  119.2 0.5 xor_add_fusion.slot_ref
  119.7 35.7 %all-to-all-done.recv_ref = bf16[8,65,32,128]{3,2,1,0:T(8,128)(2,1)} async-done(((bf16[8,65,32,128]{3,2,1,0:T(8,128)(2,1)}), bf16[8,65,32,128]{3,2,1,0:T(8,128)(2,1)}, u32[]{:S(2)}, u32[]{:S(2)}) %all-to-all-start) | async-done | bytes 4259872 | tf_op jit(solution)/shard_map/all_to_all | solution.py:248
  155.4 17.6 %conv.1 = bf16[128,32,512]{2,1,0:T(8,128)(2,1)} custom-call(s32[8]{0:T(128)} %xor_add_fusion.slot_ref, bf16[8,65,32,128]{3,2,1,0:T(8,128)(2,1)} %all-to-all-done.recv_ref, bf16[16,256,960]{2,1,0:T(8,128)(2,1)} %weights.1.w_ref), custom_call_target="tpu_custom_call" | custom-call | flops 4026531840 | bytes 16777216 | tf_op jit(solution)/shard_map/conv/pallas_call | solution.py:252
  (39 shorter events, 0.2 us)
Async XLA Ops:
  0.0 108.9 %copy-start = (s32[128,8]{0,1:T(8,128)S(1)}, s32[128,8]{0,1:T(8,128)}, u32[]{:S(2)}) copy-start(s32[128,8]{0,1:T(8,128)} %param.9) | copy-start | bytes 12292
  0.8 18.6 %collective-permute-start.3 = (bf16[1,2048]{1,0:T(2,128)(2,1)S(1)}, bf16[1,2048]{1,0:T(2,128)(2,1)S(1)}, u32[]{:S(2)}, u32[]{:S(2)}) collective-permute-start(bf16[1,2048]{1,0:T(2,128)(2,1)S(1)} %get-tuple-element.23), channel_id=1, source_target_pairs={{1,0},{2,1},{3,2},{4,3},{5,4},{6,5},{7,6},{9,8},{10,9},{11,10},{12... | collective-permute-start | bytes 12296 | tf_op jit(solution)/shard_map/ppermute | solution.py:174
  2.1 17.3 %collective-permute-start.2 = (bf16[1,2048]{1,0:T(2,128)(2,1)S(1)}, bf16[1,2048]{1,0:T(2,128)(2,1)S(1)}, u32[]{:S(2)}, u32[]{:S(2)}) collective-permute-start(bf16[1,2048]{1,0:T(2,128)(2,1)S(1)} %get-tuple-element.24), channel_id=1, source_target_pairs={{0,1},{1,2},{2,3},{3,4},{4,5},{5,6},{6,7},{8,9},{9,10},{10,11},{11... | collective-permute-start | bytes 12296 | tf_op jit(solution)/shard_map/ppermute | solution.py:174
  6.7 11.9 %copy-start.2 = (bf16[512,256]{1,0:T(8,128)(2,1)S(1)}, bf16[512,256]{1,0:T(8,128)(2,1)}, u32[]{:S(2)}) copy-start(bf16[512,256]{1,0:T(8,128)(2,1)} %param.7) | copy-start | bytes 786436
  6.7 12.7 %copy-start.1 = (bf16[512,2048]{1,0:T(8,128)(2,1)S(1)}, bf16[512,2048]{1,0:T(8,128)(2,1)}, u32[]{:S(2)}) copy-start(bf16[512,2048]{1,0:T(8,128)(2,1)} %param.6) | copy-start | bytes 6291460
  9.0 81.5 %collective-permute-start = (bf16[128,16,128]{2,1,0:T(8,128)(2,1)}, bf16[128,16,128]{2,1,0:T(8,128)(2,1)}, u32[]{:S(2)}, u32[]{:S(2)}) collective-permute-start(bf16[128,16,128]{2,1,0:T(8,128)(2,1)} %bitcast.16), channel_id=1, source_target_pairs={{0,0},{8,10},{1,33},{9,43},{16,1},{24,11},{17,32},{25,42},{32,21},... | collective-permute-start | bytes 1572872 | tf_op jit(solution)/shard_map/ppermute | solution.py:174
  11.9 78.6 %collective-permute-start.1 = (bf16[128,16,128]{2,1,0:T(8,128)(2,1)}, bf16[128,16,128]{2,1,0:T(8,128)(2,1)}, u32[]{:S(2)}, u32[]{:S(2)}) collective-permute-start(bf16[128,16,128]{2,1,0:T(8,128)(2,1)} %bitcast.18), channel_id=1, source_target_pairs={{0,10},{8,0},{1,43},{9,33},{16,11},{24,1},{17,42},{25,32},{32,31},... | collective-permute-start | bytes 1572872 | tf_op jit(solution)/shard_map/ppermute | solution.py:174
  23.9 19.6 %collective-permute-start.6 = (bf16[2,16,128]{2,1,0:T(8,128)(2,1)}, bf16[2,16,128]{2,1,0:T(8,128)(2,1)}, u32[]{:S(2)}, u32[]{:S(2)}) collective-permute-start(bf16[2,16,128]{2,1,0:T(8,128)(2,1)} %bitcast.53), channel_id=1, source_target_pairs={{0,0},{8,10},{1,33},{9,43},{16,1},{24,11},{17,32},{25,42},{32,21},... | collective-permute-start | bytes 24584 | tf_op jit(solution)/shard_map/ppermute | solution.py:174
  29.8 16.6 %collective-permute-start.7 = (bf16[2,16,128]{2,1,0:T(8,128)(2,1)}, bf16[2,16,128]{2,1,0:T(8,128)(2,1)}, u32[]{:S(2)}, u32[]{:S(2)}) collective-permute-start(bf16[2,16,128]{2,1,0:T(8,128)(2,1)} %bitcast.52), channel_id=1, source_target_pairs={{0,10},{8,0},{1,43},{9,33},{16,11},{24,1},{17,42},{25,32},{32,31},... | collective-permute-start | bytes 24584 | tf_op jit(solution)/shard_map/ppermute | solution.py:174
  31.9 14.5 %collective-permute-start.8 = (bf16[2,16,128]{2,1,0:T(8,128)(2,1)S(1)}, bf16[2,16,128]{2,1,0:T(8,128)(2,1)}, u32[]{:S(2)}, u32[]{:S(2)}) collective-permute-start(bf16[2,16,128]{2,1,0:T(8,128)(2,1)S(1)} %bitcast.62), channel_id=1, source_target_pairs={{0,20},{8,30},{1,53},{9,63},{16,21},{24,31},{17,52},{25,62},{32,1}... | collective-permute-start | bytes 24584 | tf_op jit(solution)/shard_map/ppermute | solution.py:174
  37.6 15.2 %copy-start.6 = (bf16[1,2,384]{2,1,0:T(2,128)(2,1)S(1)}, bf16[1,2,384]{2,1,0:T(2,128)(2,1)}, u32[]{:S(2)}) copy-start(bf16[1,2,384]{2,1,0:T(2,128)(2,1)} %get-tuple-element.27) | copy-start | bytes 4612
  37.6 15.2 %copy-start.5 = (bf16[1,2,384]{2,1,0:T(2,128)(2,1)S(1)}, bf16[1,2,384]{2,1,0:T(2,128)(2,1)}, u32[]{:S(2)}) copy-start(bf16[1,2,384]{2,1,0:T(2,128)(2,1)} %get-tuple-element.28) | copy-start | bytes 4612
  43.5 9.9 %collective-permute-start.9 = (bf16[2,16,128]{2,1,0:T(8,128)(2,1)S(1)}, bf16[2,16,128]{2,1,0:T(8,128)(2,1)S(1)}, u32[]{:S(2)}, u32[]{:S(2)}) collective-permute-start(bf16[2,16,128]{2,1,0:T(8,128)(2,1)S(1)} %bitcast.63), channel_id=1, source_target_pairs={{0,30},{8,20},{1,63},{9,53},{16,31},{24,21},{17,62},{25,52},{32,11... | collective-permute-start | bytes 24584 | tf_op jit(solution)/shard_map/ppermute | solution.py:174
  46.4 44.1 %collective-permute-start.4 = (bf16[128,16,128]{2,1,0:T(8,128)(2,1)S(1)}, bf16[128,16,128]{2,1,0:T(8,128)(2,1)S(1)}, u32[]{:S(2)}, u32[]{:S(2)}) collective-permute-start(bf16[128,16,128]{2,1,0:T(8,128)(2,1)S(1)} %bitcast.55), channel_id=1, source_target_pairs={{0,20},{8,30},{1,53},{9,63},{16,21},{24,31},{17,52},{25,62},{32,1}... | collective-permute-start | bytes 1572872 | tf_op jit(solution)/shard_map/ppermute | solution.py:174
  46.4 44.1 %collective-permute-start.5 = (bf16[128,16,128]{2,1,0:T(8,128)(2,1)S(1)}, bf16[128,16,128]{2,1,0:T(8,128)(2,1)S(1)}, u32[]{:S(2)}, u32[]{:S(2)}) collective-permute-start(bf16[128,16,128]{2,1,0:T(8,128)(2,1)S(1)} %bitcast.54), channel_id=1, source_target_pairs={{0,30},{8,20},{1,63},{9,53},{16,31},{24,21},{17,62},{25,52},{32,11... | collective-permute-start | bytes 1572872 | tf_op jit(solution)/shard_map/ppermute | solution.py:174
  53.4 37.2 %copy-start.13 = (bf16[2,16,128]{2,1,0:T(8,128)(2,1)}, bf16[2,16,128]{2,1,0:T(8,128)(2,1)S(1)}, u32[]{:S(2)}) copy-start(bf16[2,16,128]{2,1,0:T(8,128)(2,1)S(1)} %collective-permute-done.9.refs_7_) | copy-start | bytes 24580
  53.4 19.0 %collective-permute-start.10 = (bf16[130,3,128]{2,1,0:T(4,128)(2,1)S(1)}, bf16[130,3,128]{2,1,0:T(4,128)(2,1)S(1)}, u32[]{:S(2)}, u32[]{:S(2)}) collective-permute-start(bf16[130,3,128]{2,1,0:T(4,128)(2,1)S(1)} %pad_maximum_fusion), channel_id=1, source_target_pairs={{16,0},{17,33},{48,1},{49,32},{80,6},{81,39},{112,7},{113,38},{144... | collective-permute-start | bytes 299528 | tf_op jit(solution)/shard_map/ppermute | solution.py:174
  72.4 18.2 %copy-start.9 = (bf16[130,3,128]{2,1,0:T(4,128)(2,1)}, bf16[130,3,128]{2,1,0:T(4,128)(2,1)S(1)}, u32[]{:S(2)}) copy-start(bf16[130,3,128]{2,1,0:T(4,128)(2,1)S(1)} %collective-permute-done.10.refs_8_) | copy-start | bytes 299524
  72.4 4.0 %collective-permute-start.11 = (bf16[130,3,128]{2,1,0:T(4,128)(2,1)S(1)}, bf16[130,3,128]{2,1,0:T(4,128)(2,1)S(1)}, u32[]{:S(2)}, u32[]{:S(2)}) collective-permute-start(bf16[130,3,128]{2,1,0:T(4,128)(2,1)S(1)} %pad_maximum_fusion.1), channel_id=1, source_target_pairs={{16,10},{17,43},{48,11},{49,42},{80,8},{81,41},{112,9},{113,40},{1... | collective-permute-start | bytes 299528 | tf_op jit(solution)/shard_map/ppermute | solution.py:174
  76.3 14.2 %copy-start.10 = (bf16[130,3,128]{2,1,0:T(4,128)(2,1)}, bf16[130,3,128]{2,1,0:T(4,128)(2,1)S(1)}, u32[]{:S(2)}) copy-start(bf16[130,3,128]{2,1,0:T(4,128)(2,1)S(1)} %collective-permute-done.11.refs_9_) | copy-start | bytes 299524
  76.3 3.8 %collective-permute-start.13 = (bf16[130,3,128]{2,1,0:T(4,128)(2,1)S(1)}, bf16[130,3,128]{2,1,0:T(4,128)(2,1)S(1)}, u32[]{:S(2)}, u32[]{:S(2)}) collective-permute-start(bf16[130,3,128]{2,1,0:T(4,128)(2,1)S(1)} %pad_maximum_fusion.3), channel_id=1, source_target_pairs={{16,30},{17,63},{48,31},{49,62},{80,28},{81,61},{112,29},{113,60},... | collective-permute-start | bytes 299528 | tf_op jit(solution)/shard_map/ppermute | solution.py:174
  80.1 10.4 %copy-start.11 = (bf16[130,3,128]{2,1,0:T(4,128)(2,1)}, bf16[130,3,128]{2,1,0:T(4,128)(2,1)S(1)}, u32[]{:S(2)}) copy-start(bf16[130,3,128]{2,1,0:T(4,128)(2,1)S(1)} %collective-permute-done.13.refs_11_) | copy-start | bytes 299524
  80.1 10.3 %collective-permute-start.12 = (bf16[130,3,128]{2,1,0:T(4,128)(2,1)S(1)}, bf16[130,3,128]{2,1,0:T(4,128)(2,1)S(1)}, u32[]{:S(2)}, u32[]{:S(2)}) collective-permute-start(bf16[130,3,128]{2,1,0:T(4,128)(2,1)S(1)} %pad_maximum_fusion.2), channel_id=1, source_target_pairs={{16,20},{17,53},{48,21},{49,52},{80,18},{81,51},{112,19},{113,50},... | collective-permute-start | bytes 299528 | tf_op jit(solution)/shard_map/ppermute | solution.py:174
  90.5 0.7 copy-start.12
  90.5 0.8 copy-start.7
  90.5 1.0 copy-start.8
  99.8 8.0 %copy-start.4 = (s32[4096]{0:T(1024)S(1)}, s32[4096]{0:T(1024)}, u32[]{:S(2)}) copy-start(s32[4096]{0:T(1024)} %param.8) | copy-start | bytes 49156
  99.8 8.2 %copy-start.3 = (bf16[2,1,3,3,32,32]{5,4,3,2,1,0:T(8,128)(2,1)S(1)}, bf16[2,1,3,3,32,32]{5,4,3,2,1,0:T(8,128)(2,1)}, u32[]{:S(2)}) copy-start(bf16[2,1,3,3,32,32]{5,4,3,2,1,0:T(8,128)(2,1)} %param.10) | copy-start | bytes 110596
  99.8 55.7 %all-to-all-start = ((bf16[8,65,32,128]{3,2,1,0:T(8,128)(2,1)}), bf16[8,65,32,128]{3,2,1,0:T(8,128)(2,1)}, u32[]{:S(2)}, u32[]{:S(2)}) async-start(bf16[8,65,32,128]{3,2,1,0:T(8,128)(2,1)} %filterbank.1), calls=%async_computation | async-start | bytes 8519680 | tf_op jit(solution)/shard_map/all_to_all | solution.py:248
